TPU v7x, 32 devices: a whole 2x2x4 slice. The times are simulated.
32 devices in a mesh: fsdp: 8 (over y, x, core), seq: 4 (over z).
Axes of the slice: x: 2, y: 2, z: 4, core: 2. Of those that a mesh axis runs over, the one named last changes fastest.
Arguments:
- inputs: bfloat16 [24, 320, 1024], P('fsdp', 'seq'), may hold values from -6 to 6
- lengths: int32 [24], P('fsdp'), may hold values from 256 to 320, as said below
- cotangent: bfloat16 [24, 320, 1024], P('fsdp', 'seq'), may hold values from -6 to 6
- attn_gain: bfloat16 [1024], P('fsdp'), may hold values from 0.25 to 1.75
- attn_shift: bfloat16 [1024], P('fsdp'), may hold values from -1 to 1
- qkv_weight: bfloat16 [1024, 3072], P('fsdp'), may hold values from -0.1875 to 0.1875
- qv_bias: bfloat16 [2048], P('fsdp'), may hold values from -0.5 to 0.5
- proj_weight: bfloat16 [1024, 1024], P('fsdp'), may hold values from -1.5 to 1.5
- proj_bias: bfloat16 [1024], P('fsdp'), may hold values from -1 to 1
- mlp_gain: bfloat16 [1024], P('fsdp'), may hold values from 0.25 to 1.75
- mlp_shift: bfloat16 [1024], P('fsdp'), may hold values from -1 to 1
- up_weight: bfloat16 [1024, 4096], P('fsdp'), may hold values from -0.1875 to 0.1875
- up_bias: bfloat16 [4096], P('fsdp'), may hold values from -1 to 1
- down_weight: bfloat16 [4096, 1024], P('fsdp'), may hold values from -0.09375 to 0.09375
- down_bias: bfloat16 [1024], P('fsdp'), may hold values from -1 to 1
Outputs:
- output: bfloat16 [24, 320, 1024], P('fsdp', 'seq')
- input_grad: bfloat16 [24, 320, 1024], P('fsdp', 'seq')
- attn_gain_grad: float32 [1024], P('fsdp')
- attn_shift_grad: float32 [1024], P('fsdp')
- query_key_value_weight_gradient: float32 [1024, 3072], P('fsdp')
- qv_bias_grad: float32 [2048], P('fsdp')
- proj_weight_grad: float32 [1024, 1024], P('fsdp')
- proj_bias_grad: float32 [1024], P('fsdp')
- mlp_gain_grad: float32 [1024], P('fsdp')
- mlp_shift_grad: float32 [1024], P('fsdp')
- up_weight_grad: float32 [1024, 4096], P('fsdp')
- up_bias_grad: float32 [4096], P('fsdp')
- down_weight_grad: float32 [4096, 1024], P('fsdp')
- down_bias_grad: float32 [1024], P('fsdp')
Inputs may be any that keep to these rules, and one draw needn't show every extreme that they name: `lengths`: valid slots of each sequence; slots at or past it are padding; some sequence is full and some has the fewest.
All inputs are finite; a program needn't handle non-finite values.
Results may differ from a plain program's by a relative error of at most 0.015.
Values may be sent and summed in bfloat16 or wider, within the bound.
No kernel may reach another device: no remote copies, remote signals or barrier semaphores. Data moves between devices by JAX's collectives and lax.ppermute only.
A program may use at most 192 MiB of HBM per device.

v0:
```python
import jax
import jax.numpy as jnp
from jax import lax
from jax.sharding import PartitionSpec as P

HEAD = 64
EPSILON = 1e-06
MASKED = -1e30


def layer_norm(value_entries, norm_gain, norm_shift):
    center = value_entries - jnp.mean(value_entries, axis=-1, keepdims=True)
    inverse = lax.rsqrt(jnp.mean(center * center, axis=-1, keepdims=True) + EPSILON)
    normed = center * inverse
    return (normed * norm_gain + norm_shift, normed, inverse)


def norm_back(upstream, normed, inverse, norm_gain):
    scaled = upstream * norm_gain
    return inverse * (
        scaled
        - jnp.mean(scaled, axis=-1, keepdims=True)
        - normed * jnp.mean(scaled * normed, axis=-1, keepdims=True)
    )


def matrix_product(form, left, right):
    return jnp.einsum(form, left, right, preferred_element_type=jnp.float32)


def masked_scores(queries, key_rows, key_valid):
    raw_scores = matrix_product("sqhe,skhe->shqk", queries, key_rows) * HEAD ** (-0.5)
    return jnp.where(key_valid[:, None, None, :], raw_scores, MASKED)


def column_sums(value_entries):
    return jnp.sum(value_entries, axis=(0, 1), dtype=jnp.float32)


def unpack(gathered):
    return tuple(
        (member.astype(jnp.float32) if member.ndim == 1 else member for member in gathered)
    )


def per_device(
    inputs,
    lengths,
    cotangent,
    attn_gain,
    attn_shift,
    qkv_weight,
    qv_bias,
    proj_weight,
    proj_bias,
    mlp_gain,
    mlp_shift,
    up_weight,
    up_bias,
    down_weight,
    down_bias,
):
    seq_count, local_slots, model_width = inputs.shape
    groups_seq = lax.axis_size("seq")
    all_slots = local_slots * groups_seq
    head_width = model_width // groups_seq
    head_count = head_width // HEAD
    slot_start = lax.axis_index("seq") * local_slots
    positions = slot_start + jnp.arange(local_slots, dtype=jnp.int32)
    row_valid_mask = (positions[None, :] < lengths[:, None]).astype(jnp.float32)[:, :, None]
    key_valid = jnp.arange(all_slots, dtype=jnp.int32)[None, :] < lengths[:, None]
    shards = (
        attn_gain,
        attn_shift,
        qkv_weight,
        qv_bias,
        proj_weight,
        proj_bias,
        mlp_gain,
        mlp_shift,
        up_weight,
        up_bias,
        down_weight,
        down_bias,
    )
    (
        gain_attn,
        shift_attn,
        query_key_value_weight,
        bias_qv,
        output_projection_weight,
        output_projection_bias,
        gain_mlp,
        shift_mlp,
        up_projection_weight,
        up_projection_bias,
        down_projection_weight,
        down_projection_bias,
    ) = unpack(
        (
            lax.all_gather(shards[0], "fsdp", axis=0, tiled=True),
            lax.all_gather(shards[1], "fsdp", axis=0, tiled=True),
            lax.all_gather(shards[2], "fsdp", axis=0, tiled=True),
            lax.all_gather(shards[3], "fsdp", axis=0, tiled=True),
            lax.all_gather(shards[4], "fsdp", axis=0, tiled=True),
            lax.all_gather(shards[5], "fsdp", axis=0, tiled=True),
            lax.all_gather(shards[6], "fsdp", axis=0, tiled=True),
            lax.all_gather(shards[7], "fsdp", axis=0, tiled=True),
            lax.all_gather(shards[8], "fsdp", axis=0, tiled=True),
            lax.all_gather(shards[9], "fsdp", axis=0, tiled=True),
            lax.all_gather(shards[10], "fsdp", axis=0, tiled=True),
            lax.all_gather(shards[11], "fsdp", axis=0, tiled=True),
        )
    )
    value_entries = inputs.astype(jnp.float32)
    normed_attn, unit_attn, inverse_attn = layer_norm(value_entries, gain_attn, shift_attn)
    normalized_reduced = normed_attn.astype(jnp.bfloat16)
    complete_bias = jnp.concatenate(
        [bias_qv[:model_width], jnp.zeros((model_width,), jnp.float32), bias_qv[model_width:]]
    )
    query_key_value_rows = (
        matrix_product("vgp,pf->vgf", normalized_reduced, query_key_value_weight) + complete_bias
    ).astype(jnp.bfloat16)
    query_key_value_rows = query_key_value_rows.reshape(seq_count, local_slots, 3, model_width)
    heads = lax.all_to_all(query_key_value_rows, "seq", split_axis=3, concat_axis=1, tiled=True)
    queries = heads[:, :, 0].reshape(seq_count, all_slots, head_count, HEAD)
    key_rows = heads[:, :, 1].reshape(seq_count, all_slots, head_count, HEAD)
    value_rows = heads[:, :, 2].reshape(seq_count, all_slots, head_count, HEAD)
    scores = masked_scores(queries, key_rows, key_valid)
    row_max = jnp.max(scores, axis=-1, keepdims=True)
    exponent = jnp.exp(scores - row_max)
    totals = jnp.sum(exponent, axis=-1, keepdims=True)
    probs = exponent / totals
    log_total = row_max + jnp.log(totals)
    context = matrix_product("shqk,skhe->sqhe", probs.astype(jnp.bfloat16), value_rows).astype(
        jnp.bfloat16
    )
    context = context.reshape(seq_count, all_slots, head_width)
    context_row_values = lax.all_to_all(context, "seq", split_axis=1, concat_axis=2, tiled=True)
    hidden_activations = (
        value_entries
        + matrix_product("vgp,pf->vgf", context_row_values, output_projection_weight)
        + output_projection_bias
    )
    normed_mlp, unit_mlp, inverse_mlp = layer_norm(hidden_activations, gain_mlp, shift_mlp)
    normalized_feedforward_reduced = normed_mlp.astype(jnp.bfloat16)
    preactivation_values = (
        matrix_product("bux,xa->bua", normalized_feedforward_reduced, up_projection_weight)
        + up_projection_bias
    )
    activation_reduced = jax.nn.gelu(preactivation_values).astype(jnp.bfloat16)
    output = (
        row_valid_mask
        * (
            hidden_activations
            + matrix_product("ohq,qt->oht", activation_reduced, down_projection_weight)
            + down_projection_bias
        )
    ).astype(jnp.bfloat16)
    (
        gain_attn,
        shift_attn,
        query_key_value_weight,
        bias_qv,
        output_projection_weight,
        output_projection_bias,
        gain_mlp,
        shift_mlp,
        up_projection_weight,
        up_projection_bias,
        down_projection_weight,
        down_projection_bias,
    ) = unpack(
        (
            lax.all_gather(shards[0], "fsdp", axis=0, tiled=True),
            lax.all_gather(shards[1], "fsdp", axis=0, tiled=True),
            lax.all_gather(shards[2], "fsdp", axis=0, tiled=True),
            lax.all_gather(shards[3], "fsdp", axis=0, tiled=True),
            lax.all_gather(shards[4], "fsdp", axis=0, tiled=True),
            lax.all_gather(shards[5], "fsdp", axis=0, tiled=True),
            lax.all_gather(shards[6], "fsdp", axis=0, tiled=True),
            lax.all_gather(shards[7], "fsdp", axis=0, tiled=True),
            lax.all_gather(shards[8], "fsdp", axis=0, tiled=True),
            lax.all_gather(shards[9], "fsdp", axis=0, tiled=True),
            lax.all_gather(shards[10], "fsdp", axis=0, tiled=True),
            lax.all_gather(shards[11], "fsdp", axis=0, tiled=True),
        )
    )
    upstream = cotangent.astype(jnp.float32) * row_valid_mask
    incoming_reduced = upstream.astype(jnp.bfloat16)
    down_gradient = matrix_product("zmx,zma->xa", activation_reduced, incoming_reduced)
    down_bias_grad = column_sums(upstream)
    activation_gradient = matrix_product("jeo,xo->jex", incoming_reduced, down_projection_weight)
    preactivation_gradient = jax.vjp(jax.nn.gelu, preactivation_values)[1](activation_gradient)[
        0
    ].astype(jnp.bfloat16)
    up_projection_gradient = matrix_product(
        "znb,zng->bg", normalized_feedforward_reduced, preactivation_gradient
    )
    up_bias_grad = column_sums(preactivation_gradient)
    normalized_gradient = matrix_product(
        "ikh,th->ikt", preactivation_gradient, up_projection_weight
    )
    mlp_gain_grad = column_sums(normalized_gradient * unit_mlp)
    mlp_shift_grad = column_sums(normalized_gradient)
    hidden_grad = upstream + norm_back(normalized_gradient, unit_mlp, inverse_mlp, gain_mlp)
    attention_gradient = hidden_grad.astype(jnp.bfloat16)
    proj_bias_grad = column_sums(attention_gradient)
    projection_gradient = matrix_product("ftk,ftj->kj", context_row_values, attention_gradient)
    context_gradient = matrix_product(
        "fgo,xo->fgx", attention_gradient, output_projection_weight
    ).astype(jnp.bfloat16)
    head_grad = lax.all_to_all(context_gradient, "seq", split_axis=2, concat_axis=1, tiled=True)
    head_grad = head_grad.reshape(seq_count, all_slots, head_count, HEAD)
    scores = masked_scores(queries, key_rows, key_valid)
    probs = jnp.exp(scores - log_total)
    probs_grad = matrix_product("sqhe,skhe->shqk", head_grad, value_rows)
    inner = jnp.sum(probs * probs_grad, axis=-1, keepdims=True)
    scores_grad = (probs * (probs_grad - inner) * HEAD ** (-0.5)).astype(jnp.bfloat16)
    query_grad = matrix_product("shqk,skhe->sqhe", scores_grad, key_rows)
    key_grad = matrix_product("shqk,sqhe->skhe", scores_grad, queries)
    value_grad = matrix_product("shqk,sqhe->skhe", probs.astype(jnp.bfloat16), head_grad)
    stacked = jnp.stack([query_grad, key_grad, value_grad], axis=2).astype(jnp.bfloat16)
    stacked = stacked.reshape(seq_count, all_slots, 3, head_width)
    query_key_value_gradient = lax.all_to_all(
        stacked, "seq", split_axis=1, concat_axis=3, tiled=True
    )
    query_key_value_gradient = query_key_value_gradient.reshape(
        seq_count, local_slots, 3 * model_width
    )
    query_key_value_weight_gradient = matrix_product(
        "ftk,ftj->kj", normalized_reduced, query_key_value_gradient
    )
    qkv_sums = column_sums(query_key_value_gradient)
    qv_bias_grad = jnp.concatenate([qkv_sums[:model_width], qkv_sums[2 * model_width :]])
    attention_normed_gradient = matrix_product(
        "fgo,xo->fgx", query_key_value_gradient, query_key_value_weight
    )
    attn_gain_grad = column_sums(attention_normed_gradient * unit_attn)
    attn_shift_grad = column_sums(attention_normed_gradient)
    input_grad = (
        hidden_grad + norm_back(attention_normed_gradient, unit_attn, inverse_attn, gain_attn)
    ).astype(jnp.bfloat16)
    shares = (
        lax.psum_scatter(attn_gain_grad, "fsdp", scatter_dimension=0, tiled=True),
        lax.psum_scatter(attn_shift_grad, "fsdp", scatter_dimension=0, tiled=True),
        lax.psum_scatter(query_key_value_weight_gradient, "fsdp", scatter_dimension=0, tiled=True),
        lax.psum_scatter(qv_bias_grad, "fsdp", scatter_dimension=0, tiled=True),
        lax.psum_scatter(projection_gradient, "fsdp", scatter_dimension=0, tiled=True),
        lax.psum_scatter(proj_bias_grad, "fsdp", scatter_dimension=0, tiled=True),
        lax.psum_scatter(mlp_gain_grad, "fsdp", scatter_dimension=0, tiled=True),
        lax.psum_scatter(mlp_shift_grad, "fsdp", scatter_dimension=0, tiled=True),
        lax.psum_scatter(up_projection_gradient, "fsdp", scatter_dimension=0, tiled=True),
        lax.psum_scatter(up_bias_grad, "fsdp", scatter_dimension=0, tiled=True),
        lax.psum_scatter(down_gradient, "fsdp", scatter_dimension=0, tiled=True),
        lax.psum_scatter(down_bias_grad, "fsdp", scatter_dimension=0, tiled=True),
    )
    summed = tuple(
        (
            lax.psum(shares[0].astype(jnp.bfloat16), "seq").astype(jnp.float32),
            lax.psum(shares[1].astype(jnp.bfloat16), "seq").astype(jnp.float32),
            lax.psum(shares[2].astype(jnp.bfloat16), "seq").astype(jnp.float32),
            lax.psum(shares[3].astype(jnp.bfloat16), "seq").astype(jnp.float32),
            lax.psum(shares[4].astype(jnp.bfloat16), "seq").astype(jnp.float32),
            lax.psum(shares[5].astype(jnp.bfloat16), "seq").astype(jnp.float32),
            lax.psum(shares[6].astype(jnp.bfloat16), "seq").astype(jnp.float32),
            lax.psum(shares[7].astype(jnp.bfloat16), "seq").astype(jnp.float32),
            lax.psum(shares[8].astype(jnp.bfloat16), "seq").astype(jnp.float32),
            lax.psum(shares[9].astype(jnp.bfloat16), "seq").astype(jnp.float32),
            lax.psum(shares[10].astype(jnp.bfloat16), "seq").astype(jnp.float32),
            lax.psum(shares[11].astype(jnp.bfloat16), "seq").astype(jnp.float32),
        )
    )
    return (output, input_grad) + summed


def solution(mesh):
    in_specs = (
        P("fsdp", "seq", None),
        P("fsdp"),
        P("fsdp", "seq", None),
        P("fsdp"),
        P("fsdp"),
        P("fsdp", None),
        P("fsdp"),
        P("fsdp", None),
        P("fsdp"),
        P("fsdp"),
        P("fsdp"),
        P("fsdp", None),
        P("fsdp"),
        P("fsdp", None),
        P("fsdp"),
    )
    out_specs = (
        P("fsdp", "seq", None),
        P("fsdp", "seq", None),
        P("fsdp"),
        P("fsdp"),
        P("fsdp", None),
        P("fsdp"),
        P("fsdp", None),
        P("fsdp"),
        P("fsdp"),
        P("fsdp"),
        P("fsdp", None),
        P("fsdp"),
        P("fsdp", None),
        P("fsdp"),
    )
    return jax.shard_map(
        per_device, mesh=mesh, in_specs=in_specs, out_specs=out_specs, check_vma=False
    )
```

profile of v0, /device:TPU:0, one launch (start us, length us, event | category | flops | bytes accessed | tf_op | source)
XLA Modules:
  0.0 826.4 jit_solution(11115464629321847686)
XLA Ops:
  10.6 10.3 %all-gather = bf16[8,1,128]{2,1,0:T(2,128)(2,1)S(1)} all-gather(bf16[1,1,128]{2,1,0:T(2,128)(2,1)} %bitcast.172), channel_id=1, replica_groups=mesh['fsdp'=8,'seq'=4] {'fsdp'}, dimensions={0}, use_global_device_ids=true | all-gather | bytes 2304 | tf_op jit(solution)/shard_map/all_gather | solution.py:101
  20.9 8.6 %all-gather.1 = bf16[8,1,128]{2,1,0:T(2,128)(2,1)S(1)} all-gather(bf16[1,1,128]{2,1,0:T(2,128)(2,1)} %bitcast.173), channel_id=1, replica_groups=mesh['fsdp'=8,'seq'=4] {'fsdp'}, dimensions={0}, use_global_device_ids=true | all-gather | bytes 2304 | tf_op jit(solution)/shard_map/all_gather | solution.py:102
  29.6 8.0 all-gather.2
  39.1 19.0 %all-gather.13.cloned.1.call-done = bf16[1024,3072]{1,0:T(8,128)(2,1)} async-done(((bf16[128,3072]{1,0:T(8,128)(2,1)}), bf16[1024,3072]{1,0:T(8,128)(2,1)}) %all-gather.13.cloned.1.call-update) | async-done | bytes 6291472 | tf_op jit(solution)/shard_map/all_gather | solution.py:103
  58.2 4.6 fusion.31
  62.8 3.5 reshape.162
  66.3 5.6 copy.73
  71.9 5.0 reshape.208
  76.9 4.6 all-to-all-start
  81.6 35.3 %all-to-all-done = bf16[4,2,92160]{2,1,0:T(2,128)(2,1)} async-done(((bf16[4,2,92160]{2,1,0:T(2,128)(2,1)}), bf16[4,2,92160]{2,1,0:T(2,128)(2,1)}, u32[]{:S(2)}, u32[]{:S(2)}) %all-to-all-start) | async-done | bytes 1474592 | tf_op jit(solution)/shard_map/all_to_all | solution.py:125
  116.9 5.8 reshape.209
  122.8 3.8 copy.75
  134.3 3.5 all-to-all-start.1
  137.9 8.6 %all-gather.3 = bf16[8,1,128]{2,1,0:T(2,128)(2,1)S(1)} all-gather(bf16[1,1,128]{2,1,0:T(2,128)(2,1)S(1)} %bitcast.174), channel_id=1, replica_groups=mesh['fsdp'=8,'seq'=4] {'fsdp'}, dimensions={0}, use_global_device_ids=true | all-gather | bytes 2304 | tf_op jit(solution)/shard_map/all_gather | solution.py:106
  146.5 7.9 all-gather.4
  154.4 8.6 %all-gather.5 = bf16[8,1,128]{2,1,0:T(2,128)(2,1)S(1)} all-gather(bf16[1,1,128]{2,1,0:T(2,128)(2,1)S(1)} %bitcast.176), channel_id=1, replica_groups=mesh['fsdp'=8,'seq'=4] {'fsdp'}, dimensions={0}, use_global_device_ids=true | all-gather | bytes 2304 | tf_op jit(solution)/shard_map/all_gather | solution.py:108
  163.0 8.2 all-gather.6
  174.2 8.0 fusion.15
  182.2 18.3 %all-gather.19.cloned.1.call-done = bf16[4096,1024]{1,0:T(8,128)(2,1)} async-done(((bf16[512,1024]{1,0:T(8,128)(2,1)}), bf16[4096,1024]{1,0:T(8,128)(2,1)}) %all-gather.19.cloned.1.call-update) | async-done | bytes 8388624 | tf_op jit(solution)/shard_map/all_gather | solution.py:111
  200.5 11.3 %convert_reduce_fusion = (f32[4096]{0:T(1024)S(1)}, bf16[3,80,4096]{2,1,0:T(8,128)(2,1)S(1)}) fusion(f32[3,80,4096]{2,1,0:T(8,128)} %fusion.15, bf16[4096,1024]{1,0:T(8,128)(2,1)} %all-gather.19.cloned.1.call-done, bf16[3,80,1024]{2,1,0:T(8,128)(2,1)S(1)} %copy-done.13, f32[3,80]{1,0:T(4,128)S(1)} %compare_convert_fusion), kind=kOutput, calls=%fused_computation.35 | convolution fusion | flops 2035625984 | bytes 14795712 | tf_op jit(solution)/shard_map/jeo,xo->jex/dot_general | solution.py:28
  211.9 2.8 multiply_reduce_fusion.1
  215.1 2.8 convolution_bitcast_fusion.3
  218.0 3.1 fusion.83
  224.9 4.6 all-to-all-start.2
  229.8 14.1 %all-to-all-done.2 = bf16[4,2,30720]{2,1,0:T(2,128)(2,1)} async-done(((bf16[4,2,30720]{2,1,0:T(2,128)(2,1)}), bf16[4,2,30720]{2,1,0:T(2,128)(2,1)}, u32[]{:S(2)}, u32[]{:S(2)}) %all-to-all-start.2) | async-done | bytes 491552 | tf_op jit(solution)/shard_map/all_to_all | solution.py:213
  249.9 3.7 fusion.62
  255.5 4.6 fusion.117
  260.1 10.5 %fusion.65 = bf16[3,4,64,320]{3,2,1,0:T(8,128)(2,1)S(1)} fusion(bf16[3,320,4,64]{1,3,2,0:T(8,128)(2,1)S(1)} %bitcast.143, f32[3,4,320,320]{2,3,1,0:T(8,128)} %fusion.117, f32[3,4,320,320]{2,3,1,0:T(8,128)} %copy-done, f32[3,4,320]{2,1,0:T(4,128)S(1)} %log_add_fusion), kind=kOutput, calls=%fused_computation.61 | convolution fusion | flops 166137920 | bytes 10828800 | tf_op jit(solution)/shard_map/shqk,skhe->sqhe/dot_general | solution.py:28
  272.7 11.4 %fusion.68 = bf16[3,4,64,320]{3,2,1,0:T(8,128)(2,1)} fusion(bf16[3,320,4,64]{1,3,2,0:T(8,128)(2,1)} %bitcast.141, f32[3,4,320,320]{2,3,1,0:T(8,128)} %fusion.117, f32[3,4,320,320]{2,3,1,0:T(8,128)} %copy-done, f32[3,4,320]{2,1,0:T(4,128)S(1)} %log_add_fusion), kind=kOutput, calls=%fused_computation.62 | convolution fusion | flops 166137920 | bytes 10828800 | tf_op jit(solution)/shard_map/shqk,sqhe->skhe/dot_general | solution.py:28
  284.1 3.1 copy.89
  287.2 4.5 pad_maximum_fusion
  291.7 48.1 %all_to_all.66 = bf16[3,320,3,256]{3,2,0,1:T(4,128)(2,1)S(1)} all-to-all(bf16[3,320,3,256]{3,2,0,1:T(4,128)(2,1)S(1)} %pad_maximum_fusion), channel_id=1, replica_groups=mesh['fsdp'=8,'seq'=4] {'seq'}, dimensions={1} | all-to-all | bytes 2949120 | tf_op jit(solution)/shard_map/all_to_all | solution.py:225
  341.9 3.9 reshape.165
  345.8 8.0 convolution_bitcast_fusion.2
  353.9 14.7 %convolution_bitcast_fusion = f32[4096,1024]{1,0:T(8,128)} fusion(bf16[3,80,1024]{2,1,0:T(8,128)(2,1)} %param.17, f32[3,80]{1,0:T(4,128)S(1)} %compare_convert_fusion, f32[3,80,4096]{2,1,0:T(8,128)} %fusion.15), kind=kOutput, calls=%fused_computation.1 | convolution fusion | flops 2022850560 | bytes 21201856 | tf_op jit(solution)/shard_map/zmx,zma->xa/dot_general | solution.py:28
  368.7 10.2 %convolution_bitcast_fusion.1 = f32[1024,4096]{1,0:T(8,128)} fusion(bf16[3,80,4096]{2,1,0:T(8,128)(2,1)} %copy-done.11, f32[3,80,1024]{2,1,0:T(8,128)S(1)} %get-tuple-element.55, f32[1024]{0:T(1024)S(1)} %bitcast.158, f32[1024]{0:T(1024)S(1)} %bitcast.156, f32[3,80]{1,0:T(4,128)S(1)} %add_rsqrt_fusion, f32[3,80]{1,0:T(4,128)S(1)} %broadcast_multiply_fusion.4), kind=kOutput, calls=%fused_computation.2 | convolution fusion | flops 2014494720 | bytes 19736448 | tf_op jit(solution)/shard_map/znb,zng->bg/dot_general | solution.py:28
  380.8 63.7 %reduce-scatter.5.cloned.1.call-done = f32[128,3072]{1,0:T(8,128)} async-done(((f32[1024,3072]{1,0:T(8,128)}), f32[128,3072]{1,0:T(8,128)}) %reduce-scatter.5.cloned.1.call-update) | async-done | bytes 1572880 | tf_op jit(solution)/shard_map/reduce_scatter | solution.py:247
  446.9 117.6 %reduce-scatter.11.cloned.1.call-done = f32[512,1024]{1,0:T(8,128)} async-done(((f32[4096,1024]{1,0:T(8,128)}), f32[512,1024]{1,0:T(8,128)}) %reduce-scatter.11.cloned.1.call-update) | async-done | bytes 2097168 | tf_op jit(solution)/shard_map/reduce_scatter | solution.py:255
  564.5 2.7 convert_element_type.217
  567.2 117.2 %reduce-scatter.9.cloned.1.call-done = f32[128,4096]{1,0:T(8,128)} async-done(((f32[1024,4096]{1,0:T(8,128)}), f32[128,4096]{1,0:T(8,128)}) %reduce-scatter.9.cloned.1.call-update) | async-done | bytes 2097168 | tf_op jit(solution)/shard_map/reduce_scatter | solution.py:253
  684.4 2.7 convert_element_type.212
  689.7 8.8 %all-gather.7 = bf16[8,1,128]{2,1,0:T(2,128)(2,1)S(1)} all-gather(bf16[1,1,128]{2,1,0:T(2,128)(2,1)S(1)} %bitcast.177), channel_id=1, replica_groups=mesh['fsdp'=8,'seq'=4] {'fsdp'}, dimensions={0}, use_global_device_ids=true | all-gather | bytes 2304 | tf_op jit(solution)/shard_map/all_gather | solution.py:112
  698.5 8.1 fusion.80
  706.9 5.0 fusion.99
  712.0 25.7 %all-reduce.8 = (bf16[1024]{0:T(1024)(128)(2,1)S(1)}, bf16[1024]{0:T(1024)(128)(2,1)S(1)}, bf16[2048]{0:T(1024)(128)(2,1)S(1)}, bf16[1024]{0:T(1024)(128)(2,1)S(...) all-reduce(f32[1024]{0:T(1024)S(1)} %get-tuple-element.16, ...), channel_id=2, replica_groups=mesh['fsdp'=8,'seq'=4] {'fsdp'}, use_global_device_ids=true, to_apply=%region_12.13.clone | all-reduce | flops 12288 | bytes 73728
  738.3 12.4 %all-reduce.9 = (bf16[128]{0:T(256)(128)(2,1)S(1)}, bf16[128]{0:T(256)(128)(2,1)S(1)}, bf16[256]{0:T(256)(128)(2,1)S(1)}, bf16[128]{0:T(256)(128)(2,1)S(1)}, bf1...) all-reduce(bf16[128]{0:T(256)(128)(2,1)S(1)} %dynamic-slice.31, ...), channel_id=1, replica_groups=mesh['fsdp'=8,'seq'=4] {'seq'}, use_global_device_ids=true, to_apply=%region_13.14 | all-reduce | flops 1536 | bytes 6144 | tf_op jit(solution)/shard_map/psum | solution.py:260
  756.0 55.0 %all-reduce.13.cloned.1.call-done = (bf16[128,3072]{1,0:T(8,128)(2,1)}, bf16[128,1024]{1,0:T(8,128)(2,1)}, bf16[128,4096]{1,0:T(8,128)(2,1)}, bf16[512,1024]{1,0:T(8,128)(2,1)}) async-done(((bf16[128,3072]{1,0:T(8,128)(2,1)}, bf16[128,1024]{1,0:T(8,128)(2,1)}, bf16[128,4096]{1,0:T(8,128)(2,1)}, bf16[512,1024]{1,0:T(8,128)(2,1)}), (bf16[128,3072]{1,0:T(8,128)(2,1)}, bf16[128,1024]{1,0:T(8,128)(2,1)}, ...) | async-done | bytes 3145744 | tf_op jit(solution)/shard_map/psum | solution.py:262
  815.4 2.8 convert_element_type.213
  (141 shorter events, 49.4 us)
Async XLA Ops:
  7.2 31.7 %copy-start.1 = (bf16[3,80,1024]{2,1,0:T(8,128)(2,1)S(1)}, bf16[3,80,1024]{2,1,0:T(8,128)(2,1)}, u32[]{:S(2)}) copy-start(bf16[3,80,1024]{2,1,0:T(8,128)(2,1)} %param.15) | copy-start | bytes 1474564
  7.2 51.0 %all-gather.13.cloned.1.call-start = ((), (), s32[]{:S(2)}) async-start(), calls=%async_computation.8 | async-start | bytes 7077888 | tf_op jit(solution)/shard_map/all_gather | solution.py:103
  7.9 163.5 %all-gather.15.cloned.1.call-start = ((), (), s32[]{:S(2)}) async-start(), calls=%async_computation.9 | async-start | bytes 2359296 | tf_op jit(solution)/shard_map/all_gather | solution.py:105
  8.7 165.5 %all-gather.17.cloned.1.call-start = ((), (), s32[]{:S(2)}) async-start(), calls=%async_computation.10 | async-start | bytes 9437184 | tf_op jit(solution)/shard_map/all_gather | solution.py:109
  9.4 191.1 %all-gather.19.cloned.1.call-start = ((), (), s32[]{:S(2)}) async-start(), calls=%async_computation.11 | async-start | bytes 9437184 | tf_op jit(solution)/shard_map/all_gather | solution.py:111
  71.9 9.7 %copy-start.14 = (s32[3]{0:T(128)S(1)}, s32[3]{0:T(128)}, u32[]{:S(2)}) copy-start(s32[3]{0:T(128)} %param.16) | copy-start | bytes 40
  76.9 40.0 %all-to-all-start = ((bf16[4,2,92160]{2,1,0:T(2,128)(2,1)}), bf16[4,2,92160]{2,1,0:T(2,128)(2,1)}, u32[]{:S(2)}, u32[]{:S(2)}) async-start(bf16[4,2,92160]{2,1,0:T(2,128)(2,1)} %reshape.208), calls=%async_computation | async-start | bytes 2949120 | tf_op jit(solution)/shard_map/all_to_all | solution.py:125
  128.3 2.2 copy-start.8
  128.6 1.9 copy-start.7
  128.9 2.5 copy-start.10
  130.5 2.6 copy-start
  131.4 6.4 copy-start.15
  131.4 6.5 copy-start.16
  131.4 15.1 %copy-start.17 = (bf16[128]{0:T(256)(128)(2,1)S(1)}, bf16[128]{0:T(256)(128)(2,1)}, u32[]{:S(2)}) copy-start(bf16[128]{0:T(256)(128)(2,1)} %param.24) | copy-start | bytes 772
  131.4 22.9 %copy-start.18 = (bf16[128]{0:T(256)(128)(2,1)S(1)}, bf16[128]{0:T(256)(128)(2,1)}, u32[]{:S(2)}) copy-start(bf16[128]{0:T(256)(128)(2,1)} %param.25) | copy-start | bytes 772
  133.1 38.4 %copy-start.2 = (bf16[3,80,1024]{2,1,0:T(8,128)(2,1)S(1)}, bf16[3,80,1024]{2,1,0:T(8,128)(2,1)}, u32[]{:S(2)}) copy-start(bf16[3,80,1024]{2,1,0:T(8,128)(2,1)} %param.15) | copy-start | bytes 1474564
  134.3 37.0 %all-to-all-start.1 = ((bf16[3,320,256]{2,0,1:T(4,128)(2,1)}), bf16[3,320,256]{2,0,1:T(4,128)(2,1)S(1)}, u32[]{:S(2)}, u32[]{:S(2)}) async-start(bf16[3,320,256]{2,0,1:T(4,128)(2,1)} %copy.80), calls=%async_computation.1 | async-start | bytes 1310720 | tf_op jit(solution)/shard_map/all_to_all | solution.py:139
  137.8 241.2 %reduce-scatter.7.cloned.1.call-start = ((), (), s32[]{:S(2)}) async-start(), calls=%async_computation.13 | async-start | bytes 4718592 | tf_op jit(solution)/shard_map/reduce_scatter | solution.py:249
  174.1 26.4 %copy-start.13 = (bf16[3,80,1024]{2,1,0:T(8,128)(2,1)S(1)}, bf16[3,80,1024]{2,1,0:T(8,128)(2,1)}, u32[]{:S(2)}) copy-start(bf16[3,80,1024]{2,1,0:T(8,128)(2,1)} %param.17) | copy-start | bytes 1474564
  200.5 11.3 %copy-start.20 = (bf16[1024,4096]{1,0:T(8,128)(2,1)S(1)}, bf16[1024,4096]{1,0:T(8,128)(2,1)}, u32[]{:S(2)}) copy-start(bf16[1024,4096]{1,0:T(8,128)(2,1)} %all-gather.17.cloned.1.call-done) | copy-start | bytes 25165828
  211.8 2.8 copy-start.11
  224.9 18.9 %all-to-all-start.2 = ((bf16[4,2,30720]{2,1,0:T(2,128)(2,1)}), bf16[4,2,30720]{2,1,0:T(2,128)(2,1)}, u32[]{:S(2)}, u32[]{:S(2)}) async-start(bf16[4,2,30720]{2,1,0:T(2,128)(2,1)} %reshape.210), calls=%async_computation.2 | async-start | bytes 983040 | tf_op jit(solution)/shard_map/all_to_all | solution.py:213
  229.5 215.0 %reduce-scatter.5.cloned.1.call-start = ((), (), s32[]{:S(2)}) async-start(), calls=%async_computation.12 | async-start | bytes 14155776 | tf_op jit(solution)/shard_map/reduce_scatter | solution.py:247
  255.5 4.6 copy-start.9
  272.7 14.5 %copy-start.6 = (bf16[3,320,1,256]{3,2,0,1:T(2,128)(2,1)S(1)}, bf16[3,320,1,256]{3,2,0,1:T(2,128)(2,1)}, u32[]{:S(2)}) copy-start(bf16[3,320,1,256]{3,2,0,1:T(2,128)(2,1)} %copy.90) | copy-start | bytes 1474564
  353.8 210.7 %reduce-scatter.11.cloned.1.call-start = ((), (), s32[]{:S(2)}) async-start(), calls=%async_computation.15 | async-start | bytes 18874368 | tf_op jit(solution)/shard_map/reduce_scatter | solution.py:255
  368.6 315.8 %reduce-scatter.9.cloned.1.call-start = ((), (), s32[]{:S(2)}) async-start(), calls=%async_computation.14 | async-start | bytes 18874368 | tf_op jit(solution)/shard_map/reduce_scatter | solution.py:253
  378.9 432.2 %all-reduce.13.cloned.1.call-start = ((), (), s32[]{:S(2)}) async-start(), calls=%async_computation.16 | async-start | bytes 6291456 | tf_op jit(solution)/shard_map/psum | solution.py:262
  567.2 120.0 %copy-start.21 = (u32[32]{0:T(128)S(1)}, u32[32]{0:T(128)}, u32[]{:S(2)}) copy-start(u32[32]{0:T(128)} %constant.44) | copy-start | bytes 388
  567.2 122.5 %copy-start.19 = (bf16[128]{0:T(256)(128)(2,1)S(1)}, bf16[128]{0:T(256)(128)(2,1)}, u32[]{:S(2)}) copy-start(bf16[128]{0:T(256)(128)(2,1)} %param.29) | copy-start | bytes 772
  698.5 8.4 %copy-start.3 = (bf16[3,80,1024]{2,1,0:T(8,128)(2,1)S(1)}, bf16[3,80,1024]{2,1,0:T(8,128)(2,1)}, u32[]{:S(2)}) copy-start(bf16[3,80,1024]{2,1,0:T(8,128)(2,1)} %param.15) | copy-start | bytes 1474564
  698.5 8.4 %copy-start.5 = (bf16[3,80,3072]{2,1,0:T(8,128)(2,1)S(1)}, bf16[3,80,3072]{2,1,0:T(8,128)(2,1)}, u32[]{:S(2)}) copy-start(bf16[3,80,3072]{2,1,0:T(8,128)(2,1)} %reshape.165) | copy-start | bytes 4423684
  706.9 47.9 %copy-start.4 = (bf16[3,80,1024]{2,1,0:T(8,128)(2,1)S(1)}, bf16[3,80,1024]{2,1,0:T(8,128)(2,1)}, u32[]{:S(2)}) copy-start(bf16[3,80,1024]{2,1,0:T(8,128)(2,1)} %param.15) | copy-start | bytes 1474564
  811.1 7.1 copy-start.12
Sparse Core Ops, SparseCore 0:
  9.9 48.2 all-gather.12
  60.1 27.8 all-gather.14
  89.9 54.3 all-gather.16
  146.1 54.4 all-gather.18
  218.1 51.3 reduce-scatter.6
  353.9 90.5 reduce-scatter.4
  448.5 115.9 reduce-scatter.10
  568.5 115.9 reduce-scatter.8
  688.4 122.6 all-reduce.12
where the time goes:
time: 836 us; the launch traced here: 826 us
  waiting for transfers between devices  443 us (53%)
  blocking collectives  155 us (19%)
  matrix products  114 us (14%)
  local copies, waits for them, and re-layouts  52.6 us (6%)
  other arithmetic  31.7 us (4%)
  between operations  16.5 us (2%)
  starting transfers between devices  13.2 us (2%)
    reduce_scatter x1, waiting for transfers between devices, per_device(): lax.psum_scatter(down_gradient, 'fsdp', scatter_dimension=0, tiled=True)  118 us
    reduce_scatter x1, waiting for transfers between devices, per_device(): lax.psum_scatter(up_projection_gradient, 'fsdp', scatter_dimension=0, til...  117 us
    dot_general x18, matrix products, matrix_product(): return jnp.einsum(form, left, right, preferred_element_type=jnp.float32)  114 us
    reduce_scatter x1, waiting for transfers between devices, per_device(): lax.psum_scatter(query_key_value_weight_gradient, 'fsdp', scatter_dimensi...  63.7 us
    psum x1, waiting for transfers between devices, per_device(): lax.psum(shares[2].astype(jnp.bfloat16), 'seq').astype(jnp.float32)  55 us
    all_to_all x1, blocking collectives, per_device(): lax.all_to_all(stacked, 'seq', split_axis=1, concat_axis=3, tiled=True)  48.1 us
    all_to_all x1, waiting for transfers between devices, per_device(): lax.all_to_all(query_key_value_rows, 'seq', split_axis=3, concat_axis=1,...  35.3 us
    unnamed x1, blocking collectives  25.7 us
  transfers between devices with their start and end apart: 12, of which 8 were waited for; matrix products, arithmetic and copies ran while one was open for 20% of the time, Pallas kernels for 0%

commit v1 on v0

--- a/solution.py
+++ b/solution.py
@@ -122,7 +122,12 @@
         matrix_product("vgp,pf->vgf", normalized_reduced, query_key_value_weight) + complete_bias
     ).astype(jnp.bfloat16)
     query_key_value_rows = query_key_value_rows.reshape(seq_count, local_slots, 3, model_width)
-    heads = lax.all_to_all(query_key_value_rows, "seq", split_axis=3, concat_axis=1, tiled=True)
+    heads = jnp.concatenate(
+        lax.all_to_all(
+            jnp.stack(jnp.split(query_key_value_rows, lax.axis_size("seq"), axis=3)), "seq", 0, 0
+        ),
+        axis=1,
+    )
     queries = heads[:, :, 0].reshape(seq_count, all_slots, head_count, HEAD)
     key_rows = heads[:, :, 1].reshape(seq_count, all_slots, head_count, HEAD)
     value_rows = heads[:, :, 2].reshape(seq_count, all_slots, head_count, HEAD)

time: 836 us -> 837 us (level)
  local copies, waits for them, and re-layouts: 52.6 us -> 35.2 us
  waiting for transfers between devices: 443 us -> 456 us
    all_gather x1, waiting for transfers between devices: 18.3 us -> 34.3 us  [per_device(): lax.all_gather(shards[10], 'fsdp', axis=0, tiled=True)]
    unnamed x62 -> x90, local copies, waits for them, and re-layouts: 18 us -> 7.52 us
  transfers between devices with their start and end apart: 12 -> 12, of which waited for: 8 -> 8; matrix products, arithmetic and copies ran while one was open for 20% -> 19% of each run, Pallas kernels for 0% -> 0%
where the time goes in v1:
time: 837 us; the launch traced here: 828 us
  waiting for transfers between devices  456 us (54%)
  blocking collectives  155 us (19%)
  matrix products  117 us (14%)
  other arithmetic  35.6 us (4%)
  local copies, waits for them, and re-layouts  35.2 us (4%)
  between operations  16.6 us (2%)
  starting transfers between devices  13.2 us (2%)
    reduce_scatter x1, waiting for transfers between devices, per_device(): lax.psum_scatter(down_gradient, 'fsdp', scatter_dimension=0, tiled=True)  118 us
    reduce_scatter x1, waiting for transfers between devices, per_device(): lax.psum_scatter(up_projection_gradient, 'fsdp', scatter_dimension=0, til...  117 us
    dot_general x18, matrix products, matrix_product(): return jnp.einsum(form, left, right, preferred_element_type=jnp.float32)  117 us
    reduce_scatter x1, waiting for transfers between devices, per_device(): lax.psum_scatter(query_key_value_weight_gradient, 'fsdp', scatter_dimensi...  62.3 us
    psum x1, waiting for transfers between devices, per_device(): lax.psum(shares[2].astype(jnp.bfloat16), 'seq').astype(jnp.float32)  54.9 us
    all_to_all x1, blocking collectives, per_device(): lax.all_to_all(stacked, 'seq', split_axis=1, concat_axis=3, tiled=True)  47.9 us
    all_to_all x1, waiting for transfers between devices, per_device(): lax.all_to_all(jnp.stack(jnp.split(query_key_value_rows, lax.axis_size('s...  35.2 us
    all_gather x1, waiting for transfers between devices, per_device(): lax.all_gather(shards[10], 'fsdp', axis=0, tiled=True)  34.3 us
  transfers between devices with their start and end apart: 12, of which 8 were waited for; matrix products, arithmetic and copies ran while one was open for 19% of the time, Pallas kernels for 0%

profile of v1, /device:TPU:0, one launch (start us, length us, event | category | flops | bytes accessed | tf_op | source)
XLA Modules:
  0.0 828.4 jit_solution(4525579459065572688)
XLA Ops:
  10.6 10.3 %all-gather = bf16[8,1,128]{2,1,0:T(2,128)(2,1)S(1)} all-gather(bf16[1,1,128]{2,1,0:T(2,128)(2,1)} %bitcast.174), channel_id=1, replica_groups=mesh['fsdp'=8,'seq'=4] {'fsdp'}, dimensions={0}, use_global_device_ids=true | all-gather | bytes 2304 | tf_op jit(solution)/shard_map/all_gather | solution.py:101
  20.9 8.6 %all-gather.1 = bf16[8,1,128]{2,1,0:T(2,128)(2,1)S(1)} all-gather(bf16[1,1,128]{2,1,0:T(2,128)(2,1)} %bitcast.175), channel_id=1, replica_groups=mesh['fsdp'=8,'seq'=4] {'fsdp'}, dimensions={0}, use_global_device_ids=true | all-gather | bytes 2304 | tf_op jit(solution)/shard_map/all_gather | solution.py:102
  29.6 8.0 all-gather.2
  39.2 19.0 %all-gather.13.cloned.1.call-done = bf16[1024,3072]{1,0:T(8,128)(2,1)} async-done(((bf16[128,3072]{1,0:T(8,128)(2,1)}), bf16[1024,3072]{1,0:T(8,128)(2,1)}) %all-gather.13.cloned.1.call-update) | async-done | bytes 6291472 | tf_op jit(solution)/shard_map/all_gather | solution.py:103
  58.2 5.7 fusion.31
  63.9 4.2 reshape.168
  72.2 4.6 all-to-all-start
  76.8 35.2 %all-to-all-done = bf16[4,3,80,3,256]{4,2,3,1,0:T(8,128)(2,1)S(1)} async-done(((bf16[4,3,80,3,256]{4,2,3,1,0:T(8,128)(2,1)}), bf16[4,3,80,3,256]{4,2,3,1,0:T(8,128)(2,1)S(1)}, u32[]{:S(2)}, u32[]{:S(2)}) %all-to-all-start) | async-done | bytes 1474592 | tf_op jit(solution)/shard_map/all_to_all | solution.py:126
  118.6 3.5 all-to-all-start.1
  122.2 8.7 %all-gather.3 = bf16[8,1,128]{2,1,0:T(2,128)(2,1)S(1)} all-gather(bf16[1,1,128]{2,1,0:T(2,128)(2,1)S(1)} %bitcast.176), channel_id=1, replica_groups=mesh['fsdp'=8,'seq'=4] {'fsdp'}, dimensions={0}, use_global_device_ids=true | all-gather | bytes 2304 | tf_op jit(solution)/shard_map/all_gather | solution.py:106
  130.9 7.8 all-gather.4
  138.7 8.7 %all-gather.5 = bf16[8,1,128]{2,1,0:T(2,128)(2,1)S(1)} all-gather(bf16[1,1,128]{2,1,0:T(2,128)(2,1)S(1)} %bitcast.178), channel_id=1, replica_groups=mesh['fsdp'=8,'seq'=4] {'fsdp'}, dimensions={0}, use_global_device_ids=true | all-gather | bytes 2304 | tf_op jit(solution)/shard_map/all_gather | solution.py:108
  147.4 8.1 all-gather.6
  155.8 2.4 fusion.116
  158.5 7.7 fusion.15
  166.2 34.3 %all-gather.19.cloned.1.call-done = bf16[4096,1024]{1,0:T(8,128)(2,1)} async-done(((bf16[512,1024]{1,0:T(8,128)(2,1)}), bf16[4096,1024]{1,0:T(8,128)(2,1)}) %all-gather.19.cloned.1.call-update) | async-done | bytes 8388624 | tf_op jit(solution)/shard_map/all_gather | solution.py:111
  200.5 11.9 %convert_reduce_fusion = (f32[4096]{0:T(1024)}, bf16[3,80,4096]{2,1,0:T(8,128)(2,1)S(1)}) fusion(f32[3,80,4096]{2,1,0:T(8,128)} %fusion.15, bf16[4096,1024]{1,0:T(8,128)(2,1)} %all-gather.19.cloned.1.call-done, bf16[3,80,1024]{2,1,0:T(8,128)(2,1)S(1)} %copy-done.11, f32[3,80]{1,0:T(4,128)S(1)} %compare_convert_fusion), kind=kOutput, calls=%fused_computation.35 | convolution fusion | flops 2035625984 | bytes 14795712 | tf_op jit(solution)/shard_map/jeo,xo->jex/dot_general | solution.py:28
  212.4 3.2 multiply_reduce_fusion.1
  216.7 2.8 convolution_bitcast_fusion.3
  224.8 4.6 all-to-all-start.2
  231.0 12.6 %all-to-all-done.2 = bf16[4,2,30720]{2,1,0:T(2,128)(2,1)S(1)} async-done(((bf16[4,2,30720]{2,1,0:T(2,128)(2,1)}), bf16[4,2,30720]{2,1,0:T(2,128)(2,1)S(1)}, u32[]{:S(2)}, u32[]{:S(2)}) %all-to-all-start.2) | async-done | bytes 491552 | tf_op jit(solution)/shard_map/all_to_all | solution.py:218
  248.8 4.5 fusion.62
  253.3 2.4 copy.67
  255.7 4.5 fusion.117
  260.3 11.8 %fusion.65 = bf16[3,4,64,320]{3,2,1,0:T(8,128)(2,1)} fusion(bf16[3,320,4,64]{1,3,2,0:T(8,128)(2,1)} %bitcast.145, f32[3,4,320,320]{2,3,1,0:T(8,128)} %fusion.117, f32[3,4,320,320]{2,3,1,0:T(8,128)} %copy-done, f32[3,4,320]{2,1,0:T(4,128)} %log_add_fusion), kind=kOutput, calls=%fused_computation.62 | convolution fusion | flops 166137920 | bytes 10828800 | tf_op jit(solution)/shard_map/shqk,skhe->sqhe/dot_general | solution.py:28
  272.1 3.1 copy.65
  275.2 11.1 %fusion.68 = bf16[3,4,64,320]{3,2,1,0:T(8,128)(2,1)} fusion(bf16[3,320,4,64]{1,3,2,0:T(8,128)(2,1)S(1)} %bitcast.143, f32[3,4,320,320]{2,3,1,0:T(8,128)} %fusion.117, f32[3,4,320,320]{2,3,1,0:T(8,128)} %copy-done, f32[3,4,320]{2,1,0:T(4,128)} %log_add_fusion), kind=kOutput, calls=%fused_computation.63 | convolution fusion | flops 166137920 | bytes 10828800 | tf_op jit(solution)/shard_map/shqk,sqhe->skhe/dot_general | solution.py:28
  286.3 3.1 copy.66
  289.4 4.5 pad_maximum_fusion.1
  294.0 47.9 %all_to_all.53 = bf16[3,320,3,256]{3,2,0,1:T(4,128)(2,1)S(1)} all-to-all(bf16[3,320,3,256]{3,2,0,1:T(4,128)(2,1)S(1)} %pad_maximum_fusion.1), channel_id=1, replica_groups=mesh['fsdp'=8,'seq'=4] {'seq'}, dimensions={1} | all-to-all | bytes 2949120 | tf_op jit(solution)/shard_map/all_to_all | solution.py:230
  343.9 3.9 reshape.173
  347.8 8.0 convolution_bitcast_fusion.2
  356.5 15.1 %convolution_bitcast_fusion = f32[4096,1024]{1,0:T(8,128)} fusion(bf16[3,80,1024]{2,1,0:T(8,128)(2,1)} %param.17, f32[3,80]{1,0:T(4,128)S(1)} %copy-done.26, f32[3,80,4096]{2,1,0:T(8,128)} %fusion.15), kind=kOutput, calls=%fused_computation.1 | convolution fusion | flops 2022850560 | bytes 21201856 | tf_op jit(solution)/shard_map/zmx,zma->xa/dot_general | solution.py:28
  372.3 9.9 %convolution_bitcast_fusion.1 = f32[1024,4096]{1,0:T(8,128)} fusion(bf16[3,80,4096]{2,1,0:T(8,128)(2,1)} %copy-done.9, f32[3,80,1024]{2,1,0:T(8,128)S(1)} %get-tuple-element.59, f32[1024]{0:T(1024)S(1)} %bitcast.160, f32[1024]{0:T(1024)S(1)} %bitcast.158, f32[3,80]{1,0:T(4,128)S(1)} %copy-done.17, f32[3,80]{1,0:T(4,128)S(1)} %copy-done.13), kind=kOutput, calls=%fused_computation.2 | convolution fusion | flops 2014494720 | bytes 19736448 | tf_op jit(solution)/shard_map/znb,zng->bg/dot_general | solution.py:28
  384.2 62.3 %reduce-scatter.5.cloned.1.call-done = f32[128,3072]{1,0:T(8,128)} async-done(((f32[1024,3072]{1,0:T(8,128)}), f32[128,3072]{1,0:T(8,128)}) %reduce-scatter.5.cloned.1.call-update) | async-done | bytes 1572880 | tf_op jit(solution)/shard_map/reduce_scatter | solution.py:252
  446.5 2.4 convert_element_type.198
  448.9 117.6 %reduce-scatter.11.cloned.1.call-done = f32[512,1024]{1,0:T(8,128)} async-done(((f32[4096,1024]{1,0:T(8,128)}), f32[512,1024]{1,0:T(8,128)}) %reduce-scatter.11.cloned.1.call-update) | async-done | bytes 2097168 | tf_op jit(solution)/shard_map/reduce_scatter | solution.py:260
  566.4 2.7 convert_element_type.217
  569.2 117.2 %reduce-scatter.9.cloned.1.call-done = f32[128,4096]{1,0:T(8,128)} async-done(((f32[1024,4096]{1,0:T(8,128)}), f32[128,4096]{1,0:T(8,128)}) %reduce-scatter.9.cloned.1.call-update) | async-done | bytes 2097168 | tf_op jit(solution)/shard_map/reduce_scatter | solution.py:258
  686.4 2.7 convert_element_type.212
  691.7 8.8 %all-gather.7 = bf16[8,1,128]{2,1,0:T(2,128)(2,1)S(1)} all-gather(bf16[1,1,128]{2,1,0:T(2,128)(2,1)S(1)} %bitcast.179), channel_id=1, replica_groups=mesh['fsdp'=8,'seq'=4] {'fsdp'}, dimensions={0}, use_global_device_ids=true | all-gather | bytes 2304 | tf_op jit(solution)/shard_map/all_gather | solution.py:112
  700.5 8.1 fusion.80
  709.0 5.1 fusion.99
  714.1 25.7 %all-reduce.8 = (bf16[1024]{0:T(1024)(128)(2,1)S(1)}, bf16[1024]{0:T(1024)(128)(2,1)S(1)}, bf16[2048]{0:T(1024)(128)(2,1)S(1)}, bf16[1024]{0:T(1024)(128)(2,1)S(...) all-reduce(f32[1024]{0:T(1024)S(1)} %get-tuple-element.16, ...), channel_id=2, replica_groups=mesh['fsdp'=8,'seq'=4] {'fsdp'}, use_global_device_ids=true, to_apply=%region_12.13.clone | all-reduce | flops 12288 | bytes 73728
  740.3 12.4 %all-reduce.9 = (bf16[128]{0:T(256)(128)(2,1)S(1)}, bf16[128]{0:T(256)(128)(2,1)S(1)}, bf16[256]{0:T(256)(128)(2,1)S(1)}, bf16[128]{0:T(256)(128)(2,1)S(1)}, bf1...) all-reduce(bf16[128]{0:T(256)(128)(2,1)S(1)} %dynamic-slice.31, ...), channel_id=1, replica_groups=mesh['fsdp'=8,'seq'=4] {'seq'}, use_global_device_ids=true, to_apply=%region_13.14 | all-reduce | flops 1536 | bytes 6144 | tf_op jit(solution)/shard_map/psum | solution.py:265
  758.1 54.9 %all-reduce.13.cloned.1.call-done = (bf16[128,3072]{1,0:T(8,128)(2,1)}, bf16[128,1024]{1,0:T(8,128)(2,1)}, bf16[128,4096]{1,0:T(8,128)(2,1)}, bf16[512,1024]{1,0:T(8,128)(2,1)}) async-done(((bf16[128,3072]{1,0:T(8,128)(2,1)}, bf16[128,1024]{1,0:T(8,128)(2,1)}, bf16[128,4096]{1,0:T(8,128)(2,1)}, bf16[512,1024]{1,0:T(8,128)(2,1)}), (bf16[128,3072]{1,0:T(8,128)(2,1)}, bf16[128,1024]{1,0:T(8,128)(2,1)}, ...) | async-done | bytes 3145744 | tf_op jit(solution)/shard_map/psum | solution.py:267
  814.9 2.4 convert_element_type.199
  817.3 2.8 convert_element_type.213
  (171 shorter events, 44.9 us)
Async XLA Ops:
  7.2 31.7 %copy-start.1 = (bf16[3,80,1024]{2,1,0:T(8,128)(2,1)S(1)}, bf16[3,80,1024]{2,1,0:T(8,128)(2,1)}, u32[]{:S(2)}) copy-start(bf16[3,80,1024]{2,1,0:T(8,128)(2,1)} %param.15) | copy-start | bytes 1474564
  7.2 51.0 %all-gather.13.cloned.1.call-start = ((), (), s32[]{:S(2)}) async-start(), calls=%async_computation.8 | async-start | bytes 7077888 | tf_op jit(solution)/shard_map/all_gather | solution.py:103
  7.9 147.8 %all-gather.15.cloned.1.call-start = ((), (), s32[]{:S(2)}) async-start(), calls=%async_computation.9 | async-start | bytes 2359296 | tf_op jit(solution)/shard_map/all_gather | solution.py:105
  8.7 149.8 %all-gather.17.cloned.1.call-start = ((), (), s32[]{:S(2)}) async-start(), calls=%async_computation.10 | async-start | bytes 9437184 | tf_op jit(solution)/shard_map/all_gather | solution.py:109
  9.4 191.1 %all-gather.19.cloned.1.call-start = ((), (), s32[]{:S(2)}) async-start(), calls=%async_computation.11 | async-start | bytes 9437184 | tf_op jit(solution)/shard_map/all_gather | solution.py:111
  38.9 19.3 %copy-start.18 = (f32[3,80]{1,0:T(4,128)}, f32[3,80]{1,0:T(4,128)S(1)}, u32[]{:S(2)}) copy-start(f32[3,80]{1,0:T(4,128)S(1)} %broadcast_multiply_fusion.5) | copy-start | bytes 2884
  39.2 19.0 %copy-start.20 = (f32[3,80]{1,0:T(4,128)}, f32[3,80]{1,0:T(4,128)S(1)}, u32[]{:S(2)}) copy-start(f32[3,80]{1,0:T(4,128)S(1)} %add_rsqrt_fusion.1) | copy-start | bytes 2884
  70.8 6.0 copy-start.29
  72.2 39.9 %all-to-all-start = ((bf16[4,3,80,3,256]{4,2,3,1,0:T(8,128)(2,1)}), bf16[4,3,80,3,256]{4,2,3,1,0:T(8,128)(2,1)S(1)}, u32[]{:S(2)}, u32[]{:S(2)}) async-start(bf16[4,3,80,3,256]{4,2,3,1,0:T(8,128)(2,1)} %copy.51), calls=%async_computation | async-start | bytes 2949120 | tf_op jit(solution)/shard_map/all_to_all | solution.py:126
  112.6 2.2 copy-start.7
  112.9 1.9 copy-start.5
  113.2 2.5 copy-start.8
  114.8 2.6 copy-start
  115.7 1.7 copy-start.14
  115.7 6.4 copy-start.30
  115.7 6.5 copy-start.31
  115.7 15.2 %copy-start.32 = (bf16[128]{0:T(256)(128)(2,1)S(1)}, bf16[128]{0:T(256)(128)(2,1)}, u32[]{:S(2)}) copy-start(bf16[128]{0:T(256)(128)(2,1)} %param.24) | copy-start | bytes 772
  115.8 22.9 %copy-start.33 = (bf16[128]{0:T(256)(128)(2,1)S(1)}, bf16[128]{0:T(256)(128)(2,1)}, u32[]{:S(2)}) copy-start(bf16[128]{0:T(256)(128)(2,1)} %param.25) | copy-start | bytes 772
  118.6 37.0 %all-to-all-start.1 = ((bf16[3,320,256]{2,0,1:T(4,128)(2,1)}), bf16[3,320,256]{2,0,1:T(4,128)(2,1)S(1)}, u32[]{:S(2)}, u32[]{:S(2)}) async-start(bf16[3,320,256]{2,0,1:T(4,128)(2,1)} %copy.57), calls=%async_computation.1 | async-start | bytes 1310720 | tf_op jit(solution)/shard_map/all_to_all | solution.py:144
  122.1 260.2 %reduce-scatter.7.cloned.1.call-start = ((), (), s32[]{:S(2)}) async-start(), calls=%async_computation.13 | async-start | bytes 4718592 | tf_op jit(solution)/shard_map/reduce_scatter | solution.py:254
  155.6 60.0 %copy-start.25 = (f32[3,80]{1,0:T(4,128)}, f32[3,80]{1,0:T(4,128)S(1)}, u32[]{:S(2)}) copy-start(f32[3,80]{1,0:T(4,128)S(1)} %compare_convert_fusion) | copy-start | bytes 2884
  158.2 57.5 %copy-start.12 = (f32[3,80]{1,0:T(4,128)}, f32[3,80]{1,0:T(4,128)S(1)}, u32[]{:S(2)}) copy-start(f32[3,80]{1,0:T(4,128)S(1)} %broadcast_multiply_fusion.4) | copy-start | bytes 2884
  158.4 57.2 %copy-start.16 = (f32[3,80]{1,0:T(4,128)}, f32[3,80]{1,0:T(4,128)S(1)}, u32[]{:S(2)}) copy-start(f32[3,80]{1,0:T(4,128)S(1)} %add_rsqrt_fusion) | copy-start | bytes 2884
  158.5 42.0 %copy-start.11 = (bf16[3,80,1024]{2,1,0:T(8,128)(2,1)S(1)}, bf16[3,80,1024]{2,1,0:T(8,128)(2,1)}, u32[]{:S(2)}) copy-start(bf16[3,80,1024]{2,1,0:T(8,128)(2,1)} %param.17) | copy-start | bytes 1474564
  200.5 11.9 %copy-start.35 = (bf16[1024,4096]{1,0:T(8,128)(2,1)S(1)}, bf16[1024,4096]{1,0:T(8,128)(2,1)}, u32[]{:S(2)}) copy-start(bf16[1024,4096]{1,0:T(8,128)(2,1)} %all-gather.17.cloned.1.call-done) | copy-start | bytes 25165828
  212.4 3.2 copy-start.9
  224.8 18.8 %all-to-all-start.2 = ((bf16[4,2,30720]{2,1,0:T(2,128)(2,1)}), bf16[4,2,30720]{2,1,0:T(2,128)(2,1)S(1)}, u32[]{:S(2)}, u32[]{:S(2)}) async-start(bf16[4,2,30720]{2,1,0:T(2,128)(2,1)} %reshape.216), calls=%async_computation.2 | async-start | bytes 983040 | tf_op jit(solution)/shard_map/all_to_all | solution.py:218
  229.4 217.1 %reduce-scatter.5.cloned.1.call-start = ((), (), s32[]{:S(2)}) async-start(), calls=%async_computation.12 | async-start | bytes 14155776 | tf_op jit(solution)/shard_map/reduce_scatter | solution.py:252
  231.0 17.8 %copy-start.15 = (f32[3,4,320]{2,1,0:T(4,128)S(1)}, f32[3,4,320]{2,1,0:T(4,128)}, u32[]{:S(2)}) copy-start(f32[3,4,320]{2,1,0:T(4,128)} %log_add_fusion) | copy-start | bytes 46084
  260.3 14.9 %copy-start.6 = (bf16[3,320,1,256]{1,3,0,2:T(8,128)(2,1)S(1)}, bf16[3,320,1,256]{1,3,0,2:T(8,128)(2,1)}, u32[]{:S(2)}) copy-start(bf16[3,320,1,256]{1,3,0,2:T(8,128)(2,1)} %copy-done.5) | copy-start | bytes 1474564
  341.8 6.0 copy-start.19
  341.8 6.0 copy-start.21
  355.8 0.7 copy-start.26
  355.8 210.6 %reduce-scatter.11.cloned.1.call-start = ((), (), s32[]{:S(2)}) async-start(), calls=%async_computation.15 | async-start | bytes 18874368 | tf_op jit(solution)/shard_map/reduce_scatter | solution.py:260
  371.6 0.7 copy-start.17
  371.6 314.8 %reduce-scatter.9.cloned.1.call-start = ((), (), s32[]{:S(2)}) async-start(), calls=%async_computation.14 | async-start | bytes 18874368 | tf_op jit(solution)/shard_map/reduce_scatter | solution.py:258
  382.2 430.8 %all-reduce.13.cloned.1.call-start = ((), (), s32[]{:S(2)}) async-start(), calls=%async_computation.16 | async-start | bytes 6291456 | tf_op jit(solution)/shard_map/psum | solution.py:267
  569.2 120.0 %copy-start.36 = (u32[32]{0:T(128)S(1)}, u32[32]{0:T(128)}, u32[]{:S(2)}) copy-start(u32[32]{0:T(128)} %constant.44) | copy-start | bytes 388
  569.2 122.5 %copy-start.34 = (bf16[128]{0:T(256)(128)(2,1)S(1)}, bf16[128]{0:T(256)(128)(2,1)}, u32[]{:S(2)}) copy-start(bf16[128]{0:T(256)(128)(2,1)} %param.29) | copy-start | bytes 772
  700.5 8.4 %copy-start.2 = (bf16[3,80,1024]{2,1,0:T(8,128)(2,1)S(1)}, bf16[3,80,1024]{2,1,0:T(8,128)(2,1)}, u32[]{:S(2)}) copy-start(bf16[3,80,1024]{2,1,0:T(8,128)(2,1)} %param.15) | copy-start | bytes 1474564
  700.5 8.4 %copy-start.4 = (bf16[3,80,3072]{2,1,0:T(8,128)(2,1)S(1)}, bf16[3,80,3072]{2,1,0:T(8,128)(2,1)}, u32[]{:S(2)}) copy-start(bf16[3,80,3072]{2,1,0:T(8,128)(2,1)} %reshape.173) | copy-start | bytes 4423684
  708.9 5.1 copy-start.22
  708.9 5.1 copy-start.23
  708.9 5.1 copy-start.24
  708.9 5.1 copy-start.27
  708.9 5.1 copy-start.28
  708.9 48.0 %copy-start.3 = (bf16[3,80,1024]{2,1,0:T(8,128)(2,1)S(1)}, bf16[3,80,1024]{2,1,0:T(8,128)(2,1)}, u32[]{:S(2)}) copy-start(bf16[3,80,1024]{2,1,0:T(8,128)(2,1)} %param.15) | copy-start | bytes 1474564
  813.0 7.1 copy-start.10
  (1 other events, 0.7 us)
Sparse Core Ops, SparseCore 0:
  9.9 48.2 all-gather.12
  60.1 27.8 all-gather.14
  89.9 54.3 all-gather.16
  146.1 54.3 all-gather.18
  219.7 51.3 reduce-scatter.6
  355.9 90.5 reduce-scatter.4
  450.5 115.9 reduce-scatter.10
  570.4 115.9 reduce-scatter.8
  690.4 122.5 all-reduce.12
